TPU v7x, 256 devices: a whole 4x4x8 slice. The times are simulated.
256 devices in a mesh: dom: 64 (over x, z, core), slab: 4 (over y).
Axes of the slice: x: 4, y: 4, z: 8, core: 2. Of those that a mesh axis runs over, the one named last changes fastest.
Arguments:
- logperm: float32 [256, 16, 64, 128], P('dom', 'slab'), may hold values from -4.2 to 4.2
- source: float32 [16, 64, 128], P('slab'), may hold values from -6 to 6
- observed: float32 [16, 64, 128], P('slab'), may hold values from -1.2 to 1.2
- brownian: float32 [256, 256], replicated, may hold values from -6 to 6
Outputs:
- particles_next: float32 [256, 16, 64, 128], P('dom', 'slab')
All inputs are finite; a program needn't handle non-finite values.
Results may differ from a plain program's by a relative error of at most 0.0003.
Values sent between devices are 32-bit elements; how exact they have to be, the bound alone decides.
No kernel may reach another device: no remote copies, remote signals or barrier semaphores. Data moves between devices by JAX's collectives and lax.ppermute only.
A program may use at most 64 MiB of HBM per device.

v0:
```python
import math
import jax
import jax.numpy as jnp
from jax import lax
from jax.sharding import PartitionSpec as P

SWEEPS = 8
misfit_weight = 1000.0


def with_halo(block, sides, width):
    for axis, dim in sides:
        count = lax.axis_size(axis)
        forward = [(i, i + 1) for i in range(count - 1)]
        backward = [(target, source) for source, target in forward]
        low = lax.ppermute(
            lax.slice_in_dim(block, block.shape[dim] - width, None, axis=dim), axis, forward
        )
        high = lax.ppermute(lax.slice_in_dim(block, 0, width, axis=dim), axis, backward)
        block = jnp.concatenate([low, block, high], axis=dim)
    return block


def neighbor_sum(core, below, above, fill):
    pad_y = jnp.pad(core, ((0, 0), (0, 0), (1, 1), (0, 0)), constant_values=fill)
    pad_z = jnp.pad(core, ((0, 0), (0, 0), (0, 0), (1, 1)), constant_values=fill)
    return below + above + pad_y[:, :, :-2] + pad_y[:, :, 2:] + pad_z[..., :-2] + pad_z[..., 2:]


def grad_field(e_core, e_below, e_above, p_core, p_below, p_above, q_core, q_below, q_above):
    summed = e_below * (p_core - p_below) * (q_core - q_below) + e_above * (p_core - p_above) * (
        q_core - q_above
    )
    for dimension in (2, 3):
        padding = [(0, 0), (0, 0), (0, 0), (0, 0)]
        padding[dimension] = (1, 1)
        e_pad = jnp.pad(e_core, padding, constant_values=1.0)
        p_pad = jnp.pad(p_core, padding)
        q_pad = jnp.pad(q_core, padding)
        extent = e_core.shape[dimension]
        for offset in (0, 2):
            e_near = lax.slice_in_dim(e_pad, offset, offset + extent, axis=dimension)
            p_near = lax.slice_in_dim(p_pad, offset, offset + extent, axis=dimension)
            q_near = lax.slice_in_dim(q_pad, offset, offset + extent, axis=dimension)
            summed = summed + e_near * (p_core - p_near) * (q_core - q_near)
    return -0.5 * e_core * summed


def on_device(logperm, source, observed, brownian):
    particles, width, rows_y, depth_z = logperm.shape
    slabs = lax.axis_size("slab")
    cells = width * slabs * rows_y * depth_z
    extended = with_halo(logperm, (("slab", 1),), 1)
    e_ext = jnp.exp(0.5 * extended)
    e_core = e_ext[:, 1:-1]
    inverse = 1.0 / neighbor_sum(e_core, e_ext[:, :-2], e_ext[:, 2:], 1.0)

    def relax_rim(rhs):
        value = inverse * rhs
        for sweep_index in range(SWEEPS - 1):
            bordered = with_halo(value, (("slab", 1),), 1)
            value = inverse * (
                rhs + e_core * neighbor_sum(value, bordered[:, :-2], bordered[:, 2:], 0.0)
            )
        return value / e_core

    pressure = relax_rim(source[None])
    misfit = misfit_weight * (pressure - observed[None])
    adjoint = relax_rim(misfit)
    states = with_halo(jnp.stack([pressure, adjoint]), (("slab", 2),), 1)
    gradient = grad_field(
        e_core,
        e_ext[:, :-2],
        e_ext[:, 2:],
        pressure,
        states[0][:, :-2],
        states[0][:, 2:],
        adjoint,
        states[1][:, :-2],
        states[1][:, 2:],
    )
    g_flat = gradient.reshape(particles, -1)
    u_cells, g_cells = (
        lax.all_to_all(
            logperm.reshape(particles, -1), "dom", split_axis=1, concat_axis=0, tiled=True
        ),
        lax.all_to_all(g_flat, "dom", split_axis=1, concat_axis=0, tiled=True),
    )
    ensemble = u_cells.shape[0]
    centre = jnp.mean(u_cells, axis=0, keepdims=True)
    spread = u_cells - centre
    partial_gram = lax.dot_general(
        spread,
        g_cells,
        (((1,), (1,)), ((), ())),
        precision=lax.Precision.HIGHEST,
        preferred_element_type=jnp.float32,
    )
    gram = lax.psum(partial_gram, ("dom", "slab"))
    step_size = ensemble / (4.0 * (cells + 1))
    mixing = -(step_size / ensemble) * gram + math.sqrt(2.0 * step_size / ensemble) * brownian
    moved = (
        centre
        + 1.25 * spread
        + lax.dot_general(
            mixing,
            spread,
            (((0,), (0,)), ((), ())),
            precision=lax.Precision.HIGHEST,
            preferred_element_type=jnp.float32,
        )
    )
    returned = lax.all_to_all(moved, "dom", split_axis=0, concat_axis=1, tiled=True)
    return returned.reshape(logperm.shape)


def solution(mesh):
    return jax.shard_map(
        on_device,
        mesh=mesh,
        in_specs=(P("dom", "slab", None, None), P("slab", None, None), P("slab", None, None), P()),
        out_specs=P("dom", "slab", None, None),
        check_vma=False,
    )
```

profile of v0, /device:TPU:1, one launch (start us, length us, event | category | flops | bytes accessed | tf_op | source)
XLA Modules:
  0.0 498.0 jit_solution(12891519340523834035)
XLA Ops:
  7.6 4.0 collective-permute-start
  11.6 1.3 collective-permute-start.1
  13.7 3.6 collective-permute-done.1
  18.9 3.2 collective-permute-start.2
  22.2 1.3 collective-permute-start.3
  24.1 3.8 collective-permute-done.3
  28.3 2.9 collective-permute-start.4
  31.2 1.3 collective-permute-start.5
  33.1 3.8 collective-permute-done.5
  37.3 2.2 collective-permute-start.6
  39.6 1.3 collective-permute-start.7
  41.5 3.8 collective-permute-done.7
  45.7 1.9 collective-permute-start.8
  47.6 1.3 collective-permute-start.9
  49.5 3.8 collective-permute-done.9
  53.7 1.9 collective-permute-start.10
  55.7 1.3 collective-permute-start.11
  57.6 3.8 collective-permute-done.11
  61.8 2.1 collective-permute-start.12
  63.9 1.3 collective-permute-start.13
  66.1 4.1 collective-permute-done.13
  70.6 1.6 collective-permute-start.14
  73.6 1.8 collective-permute-done.14
  75.3 3.9 collective-permute-done.15
  79.7 2.1 collective-permute-start.16
  84.2 3.8 collective-permute-done.17
  88.4 2.2 collective-permute-start.18
  92.6 3.8 collective-permute-done.19
  96.9 2.2 collective-permute-start.20
  101.0 3.8 collective-permute-done.21
  105.3 2.2 collective-permute-start.22
  109.4 3.8 collective-permute-done.23
  113.7 1.9 collective-permute-start.24
  117.5 3.8 collective-permute-done.25
  121.8 1.9 collective-permute-start.26
  125.7 3.8 collective-permute-done.27
  130.0 1.9 collective-permute-start.28
  131.9 1.4 collective-permute-start.29
  133.8 3.9 collective-permute-done.29
  139.1 2.6 collective-permute-start.30
  144.2 28.9 %all-to-all-start = ((f32[4,64,512]{2,0,1:T(4,128)}), f32[4,64,512]{2,0,1:T(4,128)S(1)}, u32[]{:S(2)}, u32[]{:S(2)}) async-start(f32[4,64,512]{2,0,1:T(4,128)} %copy.7), calls=%async_computation | async-start | bytes 1048576 | tf_op jit(solution)/shard_map/all_to_all | solution.py:84
  176.8 13.7 %all-to-all-done = f32[4,64,512]{2,0,1:T(4,128)S(1)} async-done(((f32[4,64,512]{2,0,1:T(4,128)}), f32[4,64,512]{2,0,1:T(4,128)S(1)}, u32[]{:S(2)}, u32[]{:S(2)}) %all-to-all-start) | async-done | bytes 524320 | tf_op jit(solution)/shard_map/all_to_all | solution.py:84
  190.4 6.3 %all-to-all-start.1 = ((f32[4,64,512]{2,0,1:T(4,128)}), f32[4,64,512]{2,0,1:T(4,128)S(1)}, u32[]{:S(2)}, u32[]{:S(2)}) async-start(f32[4,64,512]{2,0,1:T(4,128)} %copy.8), calls=%async_computation.1 | async-start | bytes 1048576 | tf_op jit(solution)/shard_map/all_to_all | solution.py:87
  197.2 16.9 %all-to-all-done.1 = f32[4,64,512]{2,0,1:T(4,128)S(1)} async-done(((f32[4,64,512]{2,0,1:T(4,128)}), f32[4,64,512]{2,0,1:T(4,128)S(1)}, u32[]{:S(2)}, u32[]{:S(2)}) %all-to-all-start.1) | async-done | bytes 524320 | tf_op jit(solution)/shard_map/all_to_all | solution.py:87
  214.2 1.3 fusion.167
  215.8 245.4 %all-reduce.36.cloned.1.call-done = f32[256,256]{1,0:T(8,128)} async-done(((f32[256,256]{1,0:T(8,128)}), f32[256,256]{1,0:T(8,128)}) %all-reduce.36.cloned.1.call-update) | async-done | bytes 262160 | tf_op jit(solution)/shard_map/psum | solution.py:99
  461.1 1.6 convolution_add_fusion
  462.9 27.3 %all_to_all.54 = f32[64,4,512]{2,1,0:T(4,128)S(1)} all-to-all(f32[64,4,512]{2,1,0:T(4,128)S(1)} %all_to_all.48), channel_id=1, replica_groups=mesh['dom'=64,'slab'=4] {'dom'}, dimensions={0} | all-to-all | bytes 1048576 | tf_op jit(solution)/shard_map/all_to_all | solution.py:113
  (83 shorter events, 36.3 us)
Async XLA Ops:
  6.5 12.0 %copy-start.1 = (f32[4,64,128]{2,1,0:T(8,128)S(1)}, f32[4,64,128]{2,1,0:T(8,128)}, u32[]{:S(2)}) copy-start(f32[4,64,128]{2,1,0:T(8,128)} %param.5) | copy-start | bytes 393220
  7.6 6.2 %collective-permute-start = (f32[4,1,64,128]{3,2,1,0:T(8,128)S(1)}, f32[4,1,64,128]{3,2,1,0:T(8,128)S(1)}, u32[]{:S(2)}, u32[]{:S(2)}) collective-permute-start(f32[4,1,64,128]{3,2,1,0:T(8,128)S(1)} %get-tuple-element.41), channel_id=1, source_target_pairs={{0,1},{1,2},{2,3},{4,5},{5,6},{6,7},{8,9},{9,10},{10,11},{12,13},{... | collective-permute-start | bytes 393224 | tf_op jit(solution)/shard_map/ppermute | solution.py:16
  11.6 5.7 %collective-permute-start.1 = (f32[4,1,64,128]{3,2,1,0:T(8,128)S(1)}, f32[4,1,64,128]{3,2,1,0:T(8,128)S(1)}, u32[]{:S(2)}, u32[]{:S(2)}) collective-permute-start(f32[4,1,64,128]{3,2,1,0:T(8,128)S(1)} %get-tuple-element.42), channel_id=1, source_target_pairs={{1,0},{2,1},{3,2},{5,4},{6,5},{7,6},{9,8},{10,9},{11,10},{13,12},{... | collective-permute-start | bytes 393224 | tf_op jit(solution)/shard_map/ppermute | solution.py:19
  18.9 5.1 %collective-permute-start.2 = (f32[4,1,64,128]{3,2,1,0:T(8,128)S(1)}, f32[4,1,64,128]{3,2,1,0:T(8,128)S(1)}, u32[]{:S(2)}, u32[]{:S(2)}) collective-permute-start(f32[4,1,64,128]{3,2,1,0:T(8,128)S(1)} %get-tuple-element.39), channel_id=1, source_target_pairs={{0,1},{1,2},{2,3},{4,5},{5,6},{6,7},{8,9},{9,10},{10,11},{12,13},{... | collective-permute-start | bytes 393224 | tf_op jit(solution)/shard_map/ppermute | solution.py:16
  22.2 5.7 %collective-permute-start.3 = (f32[4,1,64,128]{3,2,1,0:T(8,128)S(1)}, f32[4,1,64,128]{3,2,1,0:T(8,128)S(1)}, u32[]{:S(2)}, u32[]{:S(2)}) collective-permute-start(f32[4,1,64,128]{3,2,1,0:T(8,128)S(1)} %get-tuple-element.40), channel_id=1, source_target_pairs={{1,0},{2,1},{3,2},{5,4},{6,5},{7,6},{9,8},{10,9},{11,10},{13,12},{... | collective-permute-start | bytes 393224 | tf_op jit(solution)/shard_map/ppermute | solution.py:19
  28.3 4.8 collective-permute-start.4
  31.2 5.7 %collective-permute-start.5 = (f32[4,1,64,128]{3,2,1,0:T(8,128)S(1)}, f32[4,1,64,128]{3,2,1,0:T(8,128)S(1)}, u32[]{:S(2)}, u32[]{:S(2)}) collective-permute-start(f32[4,1,64,128]{3,2,1,0:T(8,128)S(1)} %get-tuple-element.38), channel_id=1, source_target_pairs={{1,0},{2,1},{3,2},{5,4},{6,5},{7,6},{9,8},{10,9},{11,10},{13,12},{... | collective-permute-start | bytes 393224 | tf_op jit(solution)/shard_map/ppermute | solution.py:19
  37.3 4.1 collective-permute-start.6
  39.6 5.7 %collective-permute-start.7 = (f32[4,1,64,128]{3,2,1,0:T(8,128)S(1)}, f32[4,1,64,128]{3,2,1,0:T(8,128)S(1)}, u32[]{:S(2)}, u32[]{:S(2)}) collective-permute-start(f32[4,1,64,128]{3,2,1,0:T(8,128)S(1)} %get-tuple-element.36), channel_id=1, source_target_pairs={{1,0},{2,1},{3,2},{5,4},{6,5},{7,6},{9,8},{10,9},{11,10},{13,12},{... | collective-permute-start | bytes 393224 | tf_op jit(solution)/shard_map/ppermute | solution.py:19
  45.7 3.9 collective-permute-start.8
  47.6 5.7 %collective-permute-start.9 = (f32[4,1,64,128]{3,2,1,0:T(8,128)S(1)}, f32[4,1,64,128]{3,2,1,0:T(8,128)S(1)}, u32[]{:S(2)}, u32[]{:S(2)}) collective-permute-start(f32[4,1,64,128]{3,2,1,0:T(8,128)S(1)} %get-tuple-element.34), channel_id=1, source_target_pairs={{1,0},{2,1},{3,2},{5,4},{6,5},{7,6},{9,8},{10,9},{11,10},{13,12},{... | collective-permute-start | bytes 393224 | tf_op jit(solution)/shard_map/ppermute | solution.py:19
  53.7 3.9 collective-permute-start.10
  55.7 5.7 %collective-permute-start.11 = (f32[4,1,64,128]{3,2,1,0:T(8,128)S(1)}, f32[4,1,64,128]{3,2,1,0:T(8,128)S(1)}, u32[]{:S(2)}, u32[]{:S(2)}) collective-permute-start(f32[4,1,64,128]{3,2,1,0:T(8,128)S(1)} %get-tuple-element.32), channel_id=1, source_target_pairs={{1,0},{2,1},{3,2},{5,4},{6,5},{7,6},{9,8},{10,9},{11,10},{13,12},{... | collective-permute-start | bytes 393224 | tf_op jit(solution)/shard_map/ppermute | solution.py:19
  61.8 17.4 %copy-start = (f32[4,64,128]{2,1,0:T(8,128)S(1)}, f32[4,64,128]{2,1,0:T(8,128)}, u32[]{:S(2)}) copy-start(f32[4,64,128]{2,1,0:T(8,128)} %param.6) | copy-start | bytes 393220
  61.8 4.3 collective-permute-start.12
  63.9 6.3 %collective-permute-start.13 = (f32[4,1,64,128]{3,2,1,0:T(8,128)S(1)}, f32[4,1,64,128]{3,2,1,0:T(8,128)S(1)}, u32[]{:S(2)}, u32[]{:S(2)}) collective-permute-start(f32[4,1,64,128]{3,2,1,0:T(8,128)S(1)} %get-tuple-element.30), channel_id=1, source_target_pairs={{1,0},{2,1},{3,2},{5,4},{6,5},{7,6},{9,8},{10,9},{11,10},{13,12},{... | collective-permute-start | bytes 393224 | tf_op jit(solution)/shard_map/ppermute | solution.py:19
  70.6 4.7 collective-permute-start.14
  72.3 7.0 %collective-permute-start.15 = (f32[4,1,64,128]{3,2,1,0:T(8,128)S(1)}, f32[4,1,64,128]{3,2,1,0:T(8,128)S(1)}, u32[]{:S(2)}, u32[]{:S(2)}) collective-permute-start(f32[4,1,64,128]{3,2,1,0:T(8,128)S(1)} %get-tuple-element.28), channel_id=1, source_target_pairs={{1,0},{2,1},{3,2},{5,4},{6,5},{7,6},{9,8},{10,9},{11,10},{13,12},{... | collective-permute-start | bytes 393224 | tf_op jit(solution)/shard_map/ppermute | solution.py:19
  79.7 4.4 collective-permute-start.16
  81.9 6.1 %collective-permute-start.17 = (f32[4,1,64,128]{3,2,1,0:T(8,128)S(1)}, f32[4,1,64,128]{3,2,1,0:T(8,128)S(1)}, u32[]{:S(2)}, u32[]{:S(2)}) collective-permute-start(f32[4,1,64,128]{3,2,1,0:T(8,128)S(1)} %get-tuple-element.26), channel_id=1, source_target_pairs={{1,0},{2,1},{3,2},{5,4},{6,5},{7,6},{9,8},{10,9},{11,10},{13,12},{... | collective-permute-start | bytes 393224 | tf_op jit(solution)/shard_map/ppermute | solution.py:19
  88.4 4.2 collective-permute-start.18
  90.7 5.7 %collective-permute-start.19 = (f32[4,1,64,128]{3,2,1,0:T(8,128)S(1)}, f32[4,1,64,128]{3,2,1,0:T(8,128)S(1)}, u32[]{:S(2)}, u32[]{:S(2)}) collective-permute-start(f32[4,1,64,128]{3,2,1,0:T(8,128)S(1)} %get-tuple-element.24), channel_id=1, source_target_pairs={{1,0},{2,1},{3,2},{5,4},{6,5},{7,6},{9,8},{10,9},{11,10},{13,12},{... | collective-permute-start | bytes 393224 | tf_op jit(solution)/shard_map/ppermute | solution.py:19
  96.9 4.1 collective-permute-start.20
  99.1 5.7 %collective-permute-start.21 = (f32[4,1,64,128]{3,2,1,0:T(8,128)S(1)}, f32[4,1,64,128]{3,2,1,0:T(8,128)S(1)}, u32[]{:S(2)}, u32[]{:S(2)}) collective-permute-start(f32[4,1,64,128]{3,2,1,0:T(8,128)S(1)} %get-tuple-element.22), channel_id=1, source_target_pairs={{1,0},{2,1},{3,2},{5,4},{6,5},{7,6},{9,8},{10,9},{11,10},{13,12},{... | collective-permute-start | bytes 393224 | tf_op jit(solution)/shard_map/ppermute | solution.py:19
  105.3 4.1 collective-permute-start.22
  107.5 5.7 %collective-permute-start.23 = (f32[4,1,64,128]{3,2,1,0:T(8,128)S(1)}, f32[4,1,64,128]{3,2,1,0:T(8,128)S(1)}, u32[]{:S(2)}, u32[]{:S(2)}) collective-permute-start(f32[4,1,64,128]{3,2,1,0:T(8,128)S(1)} %get-tuple-element.20), channel_id=1, source_target_pairs={{1,0},{2,1},{3,2},{5,4},{6,5},{7,6},{9,8},{10,9},{11,10},{13,12},{... | collective-permute-start | bytes 393224 | tf_op jit(solution)/shard_map/ppermute | solution.py:19
  113.7 3.9 collective-permute-start.24
  115.6 5.7 %collective-permute-start.25 = (f32[4,1,64,128]{3,2,1,0:T(8,128)S(1)}, f32[4,1,64,128]{3,2,1,0:T(8,128)S(1)}, u32[]{:S(2)}, u32[]{:S(2)}) collective-permute-start(f32[4,1,64,128]{3,2,1,0:T(8,128)S(1)} %get-tuple-element.18), channel_id=1, source_target_pairs={{1,0},{2,1},{3,2},{5,4},{6,5},{7,6},{9,8},{10,9},{11,10},{13,12},{... | collective-permute-start | bytes 393224 | tf_op jit(solution)/shard_map/ppermute | solution.py:19
  121.8 3.9 collective-permute-start.26
  123.8 5.7 %collective-permute-start.27 = (f32[4,1,64,128]{3,2,1,0:T(8,128)S(1)}, f32[4,1,64,128]{3,2,1,0:T(8,128)S(1)}, u32[]{:S(2)}, u32[]{:S(2)}) collective-permute-start(f32[4,1,64,128]{3,2,1,0:T(8,128)S(1)} %get-tuple-element.16), channel_id=1, source_target_pairs={{1,0},{2,1},{3,2},{5,4},{6,5},{7,6},{9,8},{10,9},{11,10},{13,12},{... | collective-permute-start | bytes 393224 | tf_op jit(solution)/shard_map/ppermute | solution.py:19
  130.0 3.9 collective-permute-start.28
  131.9 11.1 %copy-start.2 = (f32[4,4,64,128]{3,2,1,0:T(8,128)S(1)}, f32[4,4,64,128]{3,2,1,0:T(8,128)}, u32[]{:S(2)}) copy-start(f32[4,4,64,128]{3,2,1,0:T(8,128)} %param.4) | copy-start | bytes 1572868
  131.9 5.8 %collective-permute-start.29 = (f32[4,1,64,128]{3,2,1,0:T(8,128)S(1)}, f32[4,1,64,128]{3,2,1,0:T(8,128)S(1)}, u32[]{:S(2)}, u32[]{:S(2)}) collective-permute-start(f32[4,1,64,128]{3,2,1,0:T(8,128)S(1)} %get-tuple-element.14), channel_id=1, source_target_pairs={{1,0},{2,1},{3,2},{5,4},{6,5},{7,6},{9,8},{10,9},{11,10},{13,12},{... | collective-permute-start | bytes 393224 | tf_op jit(solution)/shard_map/ppermute | solution.py:19
  139.1 34.0 %collective-permute-start.30 = (f32[2,4,1,64,128]{4,3,2,1,0:T(8,128)}, f32[2,4,1,64,128]{4,3,2,1,0:T(8,128)}, u32[]{:S(2)}, u32[]{:S(2)}) collective-permute-start(f32[2,4,1,64,128]{4,3,2,1,0:T(8,128)} %get-tuple-element.11), channel_id=1, source_target_pairs={{0,1},{1,2},{2,3},{4,5},{5,6},{6,7},{8,9},{9,10},{10,11},{12,13},{... | collective-permute-start | bytes 786440 | tf_op jit(solution)/shard_map/ppermute | solution.py:16
  141.7 31.4 %collective-permute-start.31 = (f32[2,4,1,64,128]{4,3,2,1,0:T(8,128)}, f32[2,4,1,64,128]{4,3,2,1,0:T(8,128)}, u32[]{:S(2)}, u32[]{:S(2)}) collective-permute-start(f32[2,4,1,64,128]{4,3,2,1,0:T(8,128)} %get-tuple-element.12), channel_id=1, source_target_pairs={{1,0},{2,1},{3,2},{5,4},{6,5},{7,6},{9,8},{10,9},{11,10},{13,12},{... | collective-permute-start | bytes 786440 | tf_op jit(solution)/shard_map/ppermute | solution.py:19
  144.2 46.2 %all-to-all-start = ((f32[4,64,512]{2,0,1:T(4,128)}), f32[4,64,512]{2,0,1:T(4,128)S(1)}, u32[]{:S(2)}, u32[]{:S(2)}) async-start(f32[4,64,512]{2,0,1:T(4,128)} %copy.7), calls=%async_computation | async-start | bytes 1048576 | tf_op jit(solution)/shard_map/all_to_all | solution.py:84
  190.4 23.6 %all-to-all-start.1 = ((f32[4,64,512]{2,0,1:T(4,128)}), f32[4,64,512]{2,0,1:T(4,128)S(1)}, u32[]{:S(2)}, u32[]{:S(2)}) async-start(f32[4,64,512]{2,0,1:T(4,128)} %copy.8), calls=%async_computation.1 | async-start | bytes 1048576 | tf_op jit(solution)/shard_map/all_to_all | solution.py:87
  196.7 264.4 %all-reduce.36.cloned.1.call-start = ((), (), s32[]{:S(2)}) async-start(), calls=%async_computation.3 | async-start | bytes 524288 | tf_op jit(solution)/shard_map/psum | solution.py:99
  214.2 246.9 %copy-start.3 = (f32[256,256]{1,0:T(8,128)S(1)}, f32[256,256]{1,0:T(8,128)}, u32[]{:S(2)}) copy-start(f32[256,256]{1,0:T(8,128)} %param.7) | copy-start | bytes 786436
Sparse Core Ops, SparseCore 0:
  215.7 245.3 all-reduce.35
where the time goes:
time: 499 us; the launch traced here: 498 us
  waiting for transfers between devices  344 us (69%)
  starting transfers between devices  93 us (19%)
  blocking collectives  27.3 us (5%)
  between operations  14.1 us (3%)
  other arithmetic  10.8 us (2%)
  local copies, waits for them, and re-layouts  5.66 us (1%)
    psum x1, waiting for transfers between devices, on_device(): gram = lax.psum(partial_gram, ('dom', 'slab'))  245 us
    ppermute x16, waiting for transfers between devices, with_halo(): lax.ppermute(lax.slice_in_dim(block, 0, width, axis=dim), axis, backward)  57.2 us
    ppermute x16, starting transfers between devices, with_halo(): lax.ppermute(lax.slice_in_dim(block, block.shape[dim] - width, None, axis...  37 us
    all_to_all x1, starting transfers between devices, on_device(): lax.all_to_all(logperm.reshape(particles, -1), 'dom', split_axis=1, conca...  28.9 us
    all_to_all x1, blocking collectives, on_device(): lax.all_to_all(moved, 'dom', split_axis=0, concat_axis=1, tiled=True)  27.3 us
    ppermute x16, starting transfers between devices, with_halo(): lax.ppermute(lax.slice_in_dim(block, 0, width, axis=dim), axis, backward)  20.8 us
    all_to_all x1, waiting for transfers between devices, on_device(): lax.all_to_all(g_flat, 'dom', split_axis=1, concat_axis=0, tiled=True)  16.9 us
    all_to_all x1, waiting for transfers between devices, on_device(): lax.all_to_all(logperm.reshape(particles, -1), 'dom', split_axis=1, conca...  13.7 us
  transfers between devices with their start and end apart: 35, of which 33 were waited for; matrix products, arithmetic and copies ran while one was open for 1% of the time, Pallas kernels for 0%

commit v1 on v0

--- a/solution.py
+++ b/solution.py
@@ -110,7 +110,10 @@
             preferred_element_type=jnp.float32,
         )
     )
-    returned = lax.all_to_all(moved, "dom", split_axis=0, concat_axis=1, tiled=True)
+    returned = jnp.concatenate(
+        lax.all_to_all(jnp.stack(jnp.split(moved, lax.axis_size("dom"), axis=0)), "dom", 0, 0),
+        axis=1,
+    )
     return returned.reshape(logperm.shape)
 
 

time: 499 us -> 500 us (level)
  no operation moved by 1% of the time
where the time goes in v1:
time: 500 us; the launch traced here: 499 us
  waiting for transfers between devices  344 us (69%)
  starting transfers between devices  93 us (19%)
  blocking collectives  27.3 us (5%)
  between operations  14.3 us (3%)
  other arithmetic  10.8 us (2%)
  local copies, waits for them, and re-layouts  6.16 us (1%)
    psum x1, waiting for transfers between devices, on_device(): gram = lax.psum(partial_gram, ('dom', 'slab'))  245 us
    ppermute x16, waiting for transfers between devices, with_halo(): lax.ppermute(lax.slice_in_dim(block, 0, width, axis=dim), axis, backward)  57.2 us
    ppermute x16, starting transfers between devices, with_halo(): lax.ppermute(lax.slice_in_dim(block, block.shape[dim] - width, None, axis...  37 us
    all_to_all x1, starting transfers between devices, on_device(): lax.all_to_all(logperm.reshape(particles, -1), 'dom', split_axis=1, conca...  28.9 us
    all_to_all x1, blocking collectives, on_device(): lax.all_to_all(jnp.stack(jnp.split(moved, lax.axis_size('dom'), axis=0)),...  27.3 us
    ppermute x16, starting transfers between devices, with_halo(): lax.ppermute(lax.slice_in_dim(block, 0, width, axis=dim), axis, backward)  20.8 us
    all_to_all x1, waiting for transfers between devices, on_device(): lax.all_to_all(g_flat, 'dom', split_axis=1, concat_axis=0, tiled=True)  16.9 us
    all_to_all x1, waiting for transfers between devices, on_device(): lax.all_to_all(logperm.reshape(particles, -1), 'dom', split_axis=1, conca...  13.7 us
  transfers between devices with their start and end apart: 35, of which 33 were waited for; matrix products, arithmetic and copies ran while one was open for 1% of the time, Pallas kernels for 0%

profile of v1, /device:TPU:1, one launch (start us, length us, event | category | flops | bytes accessed | tf_op | source)
XLA Modules:
  0.0 498.8 jit_solution(8899087090216384197)
XLA Ops:
  7.6 4.0 collective-permute-start
  11.6 1.3 collective-permute-start.1
  13.7 3.6 collective-permute-done.1
  18.9 3.2 collective-permute-start.2
  22.2 1.3 collective-permute-start.3
  24.1 3.8 collective-permute-done.3
  28.3 2.9 collective-permute-start.4
  31.2 1.3 collective-permute-start.5
  33.1 3.8 collective-permute-done.5
  37.3 2.2 collective-permute-start.6
  39.5 1.3 collective-permute-start.7
  41.5 3.8 collective-permute-done.7
  45.6 1.9 collective-permute-start.8
  47.6 1.3 collective-permute-start.9
  49.5 3.8 collective-permute-done.9
  53.7 1.9 collective-permute-start.10
  55.6 1.3 collective-permute-start.11
  57.5 3.8 collective-permute-done.11
  61.7 2.1 collective-permute-start.12
  66.1 4.1 collective-permute-done.13
  70.6 1.6 collective-permute-start.14
  73.5 1.7 collective-permute-done.14
  75.3 3.9 collective-permute-done.15
  79.7 2.1 collective-permute-start.16
  84.1 3.8 collective-permute-done.17
  88.4 2.2 collective-permute-start.18
  92.5 3.8 collective-permute-done.19
  96.8 2.2 collective-permute-start.20
  100.9 3.8 collective-permute-done.21
  105.2 2.2 collective-permute-start.22
  107.4 1.3 collective-permute-start.23
  109.4 3.8 collective-permute-done.23
  113.6 1.9 collective-permute-start.24
  117.5 3.8 collective-permute-done.25
  121.8 1.9 collective-permute-start.26
  125.6 3.8 collective-permute-done.27
  129.9 1.9 collective-permute-start.28
  131.9 1.4 collective-permute-start.29
  133.8 3.9 collective-permute-done.29
  139.1 2.6 collective-permute-start.30
  144.2 28.9 %all-to-all-start = ((f32[4,64,512]{2,0,1:T(4,128)}), f32[4,64,512]{2,0,1:T(4,128)S(1)}, u32[]{:S(2)}, u32[]{:S(2)}) async-start(f32[4,64,512]{2,0,1:T(4,128)} %copy.6), calls=%async_computation | async-start | bytes 1048576 | tf_op jit(solution)/shard_map/all_to_all | solution.py:84
  176.8 13.7 %all-to-all-done = f32[4,64,512]{2,0,1:T(4,128)S(1)} async-done(((f32[4,64,512]{2,0,1:T(4,128)}), f32[4,64,512]{2,0,1:T(4,128)S(1)}, u32[]{:S(2)}, u32[]{:S(2)}) %all-to-all-start) | async-done | bytes 524320 | tf_op jit(solution)/shard_map/all_to_all | solution.py:84
  190.4 6.3 %all-to-all-start.1 = ((f32[4,64,512]{2,0,1:T(4,128)}), f32[4,64,512]{2,0,1:T(4,128)S(1)}, u32[]{:S(2)}, u32[]{:S(2)}) async-start(f32[4,64,512]{2,0,1:T(4,128)} %copy.7), calls=%async_computation.1 | async-start | bytes 1048576 | tf_op jit(solution)/shard_map/all_to_all | solution.py:87
  197.2 16.9 %all-to-all-done.1 = f32[4,64,512]{2,0,1:T(4,128)S(1)} async-done(((f32[4,64,512]{2,0,1:T(4,128)}), f32[4,64,512]{2,0,1:T(4,128)S(1)}, u32[]{:S(2)}, u32[]{:S(2)}) %all-to-all-start.1) | async-done | bytes 524320 | tf_op jit(solution)/shard_map/all_to_all | solution.py:87
  214.3 1.3 fusion.167
  215.8 245.4 %all-reduce.36.cloned.1.call-done = f32[256,256]{1,0:T(8,128)} async-done(((f32[256,256]{1,0:T(8,128)}), f32[256,256]{1,0:T(8,128)}) %all-reduce.36.cloned.1.call-update) | async-done | bytes 262160 | tf_op jit(solution)/shard_map/psum | solution.py:99
  461.2 1.6 convolution_add_fusion
  463.7 27.3 %all_to_all.43 = f32[64,4,512]{2,1,0:T(4,128)S(1)} all-to-all(f32[64,4,512]{2,1,0:T(4,128)S(1)} %constant_dynamic-update-slice_fusion), channel_id=1, replica_groups=mesh['dom'=64,'slab'=4] {'dom'}, dimensions={0} | all-to-all | bytes 1048576 | tf_op jit(solution)/shard_map/all_to_all | solution.py:114
  (146 shorter events, 36.8 us)
Async XLA Ops:
  6.5 12.0 %copy-start.1 = (f32[4,64,128]{2,1,0:T(8,128)S(1)}, f32[4,64,128]{2,1,0:T(8,128)}, u32[]{:S(2)}) copy-start(f32[4,64,128]{2,1,0:T(8,128)} %param.5) | copy-start | bytes 393220
  7.6 6.2 %collective-permute-start = (f32[4,1,64,128]{3,2,1,0:T(8,128)S(1)}, f32[4,1,64,128]{3,2,1,0:T(8,128)S(1)}, u32[]{:S(2)}, u32[]{:S(2)}) collective-permute-start(f32[4,1,64,128]{3,2,1,0:T(8,128)S(1)} %get-tuple-element.41), channel_id=1, source_target_pairs={{0,1},{1,2},{2,3},{4,5},{5,6},{6,7},{8,9},{9,10},{10,11},{12,13},{... | collective-permute-start | bytes 393224 | tf_op jit(solution)/shard_map/ppermute | solution.py:16
  11.6 5.7 %collective-permute-start.1 = (f32[4,1,64,128]{3,2,1,0:T(8,128)S(1)}, f32[4,1,64,128]{3,2,1,0:T(8,128)S(1)}, u32[]{:S(2)}, u32[]{:S(2)}) collective-permute-start(f32[4,1,64,128]{3,2,1,0:T(8,128)S(1)} %get-tuple-element.42), channel_id=1, source_target_pairs={{1,0},{2,1},{3,2},{5,4},{6,5},{7,6},{9,8},{10,9},{11,10},{13,12},{... | collective-permute-start | bytes 393224 | tf_op jit(solution)/shard_map/ppermute | solution.py:19
  18.9 5.1 %collective-permute-start.2 = (f32[4,1,64,128]{3,2,1,0:T(8,128)S(1)}, f32[4,1,64,128]{3,2,1,0:T(8,128)S(1)}, u32[]{:S(2)}, u32[]{:S(2)}) collective-permute-start(f32[4,1,64,128]{3,2,1,0:T(8,128)S(1)} %get-tuple-element.39), channel_id=1, source_target_pairs={{0,1},{1,2},{2,3},{4,5},{5,6},{6,7},{8,9},{9,10},{10,11},{12,13},{... | collective-permute-start | bytes 393224 | tf_op jit(solution)/shard_map/ppermute | solution.py:16
  22.2 5.7 %collective-permute-start.3 = (f32[4,1,64,128]{3,2,1,0:T(8,128)S(1)}, f32[4,1,64,128]{3,2,1,0:T(8,128)S(1)}, u32[]{:S(2)}, u32[]{:S(2)}) collective-permute-start(f32[4,1,64,128]{3,2,1,0:T(8,128)S(1)} %get-tuple-element.40), channel_id=1, source_target_pairs={{1,0},{2,1},{3,2},{5,4},{6,5},{7,6},{9,8},{10,9},{11,10},{13,12},{... | collective-permute-start | bytes 393224 | tf_op jit(solution)/shard_map/ppermute | solution.py:19
  28.3 4.8 collective-permute-start.4
  31.2 5.7 %collective-permute-start.5 = (f32[4,1,64,128]{3,2,1,0:T(8,128)S(1)}, f32[4,1,64,128]{3,2,1,0:T(8,128)S(1)}, u32[]{:S(2)}, u32[]{:S(2)}) collective-permute-start(f32[4,1,64,128]{3,2,1,0:T(8,128)S(1)} %get-tuple-element.38), channel_id=1, source_target_pairs={{1,0},{2,1},{3,2},{5,4},{6,5},{7,6},{9,8},{10,9},{11,10},{13,12},{... | collective-permute-start | bytes 393224 | tf_op jit(solution)/shard_map/ppermute | solution.py:19
  37.3 4.1 collective-permute-start.6
  39.5 5.7 %collective-permute-start.7 = (f32[4,1,64,128]{3,2,1,0:T(8,128)S(1)}, f32[4,1,64,128]{3,2,1,0:T(8,128)S(1)}, u32[]{:S(2)}, u32[]{:S(2)}) collective-permute-start(f32[4,1,64,128]{3,2,1,0:T(8,128)S(1)} %get-tuple-element.36), channel_id=1, source_target_pairs={{1,0},{2,1},{3,2},{5,4},{6,5},{7,6},{9,8},{10,9},{11,10},{13,12},{... | collective-permute-start | bytes 393224 | tf_op jit(solution)/shard_map/ppermute | solution.py:19
  45.6 3.9 collective-permute-start.8
  47.6 5.7 %collective-permute-start.9 = (f32[4,1,64,128]{3,2,1,0:T(8,128)S(1)}, f32[4,1,64,128]{3,2,1,0:T(8,128)S(1)}, u32[]{:S(2)}, u32[]{:S(2)}) collective-permute-start(f32[4,1,64,128]{3,2,1,0:T(8,128)S(1)} %get-tuple-element.34), channel_id=1, source_target_pairs={{1,0},{2,1},{3,2},{5,4},{6,5},{7,6},{9,8},{10,9},{11,10},{13,12},{... | collective-permute-start | bytes 393224 | tf_op jit(solution)/shard_map/ppermute | solution.py:19
  53.7 3.9 collective-permute-start.10
  55.6 5.7 %collective-permute-start.11 = (f32[4,1,64,128]{3,2,1,0:T(8,128)S(1)}, f32[4,1,64,128]{3,2,1,0:T(8,128)S(1)}, u32[]{:S(2)}, u32[]{:S(2)}) collective-permute-start(f32[4,1,64,128]{3,2,1,0:T(8,128)S(1)} %get-tuple-element.32), channel_id=1, source_target_pairs={{1,0},{2,1},{3,2},{5,4},{6,5},{7,6},{9,8},{10,9},{11,10},{13,12},{... | collective-permute-start | bytes 393224 | tf_op jit(solution)/shard_map/ppermute | solution.py:19
  61.7 17.4 %copy-start = (f32[4,64,128]{2,1,0:T(8,128)S(1)}, f32[4,64,128]{2,1,0:T(8,128)}, u32[]{:S(2)}) copy-start(f32[4,64,128]{2,1,0:T(8,128)} %param.6) | copy-start | bytes 393220
  61.7 4.3 collective-permute-start.12
  63.8 6.4 %collective-permute-start.13 = (f32[4,1,64,128]{3,2,1,0:T(8,128)S(1)}, f32[4,1,64,128]{3,2,1,0:T(8,128)S(1)}, u32[]{:S(2)}, u32[]{:S(2)}) collective-permute-start(f32[4,1,64,128]{3,2,1,0:T(8,128)S(1)} %get-tuple-element.30), channel_id=1, source_target_pairs={{1,0},{2,1},{3,2},{5,4},{6,5},{7,6},{9,8},{10,9},{11,10},{13,12},{... | collective-permute-start | bytes 393224 | tf_op jit(solution)/shard_map/ppermute | solution.py:19
  70.6 4.7 collective-permute-start.14
  72.2 7.0 %collective-permute-start.15 = (f32[4,1,64,128]{3,2,1,0:T(8,128)S(1)}, f32[4,1,64,128]{3,2,1,0:T(8,128)S(1)}, u32[]{:S(2)}, u32[]{:S(2)}) collective-permute-start(f32[4,1,64,128]{3,2,1,0:T(8,128)S(1)} %get-tuple-element.28), channel_id=1, source_target_pairs={{1,0},{2,1},{3,2},{5,4},{6,5},{7,6},{9,8},{10,9},{11,10},{13,12},{... | collective-permute-start | bytes 393224 | tf_op jit(solution)/shard_map/ppermute | solution.py:19
  79.7 4.4 collective-permute-start.16
  81.8 6.1 %collective-permute-start.17 = (f32[4,1,64,128]{3,2,1,0:T(8,128)S(1)}, f32[4,1,64,128]{3,2,1,0:T(8,128)S(1)}, u32[]{:S(2)}, u32[]{:S(2)}) collective-permute-start(f32[4,1,64,128]{3,2,1,0:T(8,128)S(1)} %get-tuple-element.26), channel_id=1, source_target_pairs={{1,0},{2,1},{3,2},{5,4},{6,5},{7,6},{9,8},{10,9},{11,10},{13,12},{... | collective-permute-start | bytes 393224 | tf_op jit(solution)/shard_map/ppermute | solution.py:19
  88.4 4.2 collective-permute-start.18
  90.6 5.7 %collective-permute-start.19 = (f32[4,1,64,128]{3,2,1,0:T(8,128)S(1)}, f32[4,1,64,128]{3,2,1,0:T(8,128)S(1)}, u32[]{:S(2)}, u32[]{:S(2)}) collective-permute-start(f32[4,1,64,128]{3,2,1,0:T(8,128)S(1)} %get-tuple-element.24), channel_id=1, source_target_pairs={{1,0},{2,1},{3,2},{5,4},{6,5},{7,6},{9,8},{10,9},{11,10},{13,12},{... | collective-permute-start | bytes 393224 | tf_op jit(solution)/shard_map/ppermute | solution.py:19
  96.8 4.1 collective-permute-start.20
  99.0 5.7 %collective-permute-start.21 = (f32[4,1,64,128]{3,2,1,0:T(8,128)S(1)}, f32[4,1,64,128]{3,2,1,0:T(8,128)S(1)}, u32[]{:S(2)}, u32[]{:S(2)}) collective-permute-start(f32[4,1,64,128]{3,2,1,0:T(8,128)S(1)} %get-tuple-element.22), channel_id=1, source_target_pairs={{1,0},{2,1},{3,2},{5,4},{6,5},{7,6},{9,8},{10,9},{11,10},{13,12},{... | collective-permute-start | bytes 393224 | tf_op jit(solution)/shard_map/ppermute | solution.py:19
  105.2 4.1 collective-permute-start.22
  107.4 5.7 %collective-permute-start.23 = (f32[4,1,64,128]{3,2,1,0:T(8,128)S(1)}, f32[4,1,64,128]{3,2,1,0:T(8,128)S(1)}, u32[]{:S(2)}, u32[]{:S(2)}) collective-permute-start(f32[4,1,64,128]{3,2,1,0:T(8,128)S(1)} %get-tuple-element.20), channel_id=1, source_target_pairs={{1,0},{2,1},{3,2},{5,4},{6,5},{7,6},{9,8},{10,9},{11,10},{13,12},{... | collective-permute-start | bytes 393224 | tf_op jit(solution)/shard_map/ppermute | solution.py:19
  113.6 3.9 collective-permute-start.24
  115.6 5.7 %collective-permute-start.25 = (f32[4,1,64,128]{3,2,1,0:T(8,128)S(1)}, f32[4,1,64,128]{3,2,1,0:T(8,128)S(1)}, u32[]{:S(2)}, u32[]{:S(2)}) collective-permute-start(f32[4,1,64,128]{3,2,1,0:T(8,128)S(1)} %get-tuple-element.18), channel_id=1, source_target_pairs={{1,0},{2,1},{3,2},{5,4},{6,5},{7,6},{9,8},{10,9},{11,10},{13,12},{... | collective-permute-start | bytes 393224 | tf_op jit(solution)/shard_map/ppermute | solution.py:19
  121.8 3.9 collective-permute-start.26
  123.7 5.7 %collective-permute-start.27 = (f32[4,1,64,128]{3,2,1,0:T(8,128)S(1)}, f32[4,1,64,128]{3,2,1,0:T(8,128)S(1)}, u32[]{:S(2)}, u32[]{:S(2)}) collective-permute-start(f32[4,1,64,128]{3,2,1,0:T(8,128)S(1)} %get-tuple-element.16), channel_id=1, source_target_pairs={{1,0},{2,1},{3,2},{5,4},{6,5},{7,6},{9,8},{10,9},{11,10},{13,12},{... | collective-permute-start | bytes 393224 | tf_op jit(solution)/shard_map/ppermute | solution.py:19
  129.9 3.9 collective-permute-start.28
  131.8 11.1 %copy-start.2 = (f32[4,4,64,128]{3,2,1,0:T(8,128)S(1)}, f32[4,4,64,128]{3,2,1,0:T(8,128)}, u32[]{:S(2)}) copy-start(f32[4,4,64,128]{3,2,1,0:T(8,128)} %param.4) | copy-start | bytes 1572868
  131.9 5.8 %collective-permute-start.29 = (f32[4,1,64,128]{3,2,1,0:T(8,128)S(1)}, f32[4,1,64,128]{3,2,1,0:T(8,128)S(1)}, u32[]{:S(2)}, u32[]{:S(2)}) collective-permute-start(f32[4,1,64,128]{3,2,1,0:T(8,128)S(1)} %get-tuple-element.14), channel_id=1, source_target_pairs={{1,0},{2,1},{3,2},{5,4},{6,5},{7,6},{9,8},{10,9},{11,10},{13,12},{... | collective-permute-start | bytes 393224 | tf_op jit(solution)/shard_map/ppermute | solution.py:19
  139.1 34.1 %collective-permute-start.30 = (f32[2,4,1,64,128]{4,3,2,1,0:T(8,128)}, f32[2,4,1,64,128]{4,3,2,1,0:T(8,128)}, u32[]{:S(2)}, u32[]{:S(2)}) collective-permute-start(f32[2,4,1,64,128]{4,3,2,1,0:T(8,128)} %get-tuple-element.11), channel_id=1, source_target_pairs={{0,1},{1,2},{2,3},{4,5},{5,6},{6,7},{8,9},{9,10},{10,11},{12,13},{... | collective-permute-start | bytes 786440 | tf_op jit(solution)/shard_map/ppermute | solution.py:16
  141.7 31.5 %collective-permute-start.31 = (f32[2,4,1,64,128]{4,3,2,1,0:T(8,128)}, f32[2,4,1,64,128]{4,3,2,1,0:T(8,128)}, u32[]{:S(2)}, u32[]{:S(2)}) collective-permute-start(f32[2,4,1,64,128]{4,3,2,1,0:T(8,128)} %get-tuple-element.12), channel_id=1, source_target_pairs={{1,0},{2,1},{3,2},{5,4},{6,5},{7,6},{9,8},{10,9},{11,10},{13,12},{... | collective-permute-start | bytes 786440 | tf_op jit(solution)/shard_map/ppermute | solution.py:19
  144.2 46.3 %all-to-all-start = ((f32[4,64,512]{2,0,1:T(4,128)}), f32[4,64,512]{2,0,1:T(4,128)S(1)}, u32[]{:S(2)}, u32[]{:S(2)}) async-start(f32[4,64,512]{2,0,1:T(4,128)} %copy.6), calls=%async_computation | async-start | bytes 1048576 | tf_op jit(solution)/shard_map/all_to_all | solution.py:84
  190.4 23.6 %all-to-all-start.1 = ((f32[4,64,512]{2,0,1:T(4,128)}), f32[4,64,512]{2,0,1:T(4,128)S(1)}, u32[]{:S(2)}, u32[]{:S(2)}) async-start(f32[4,64,512]{2,0,1:T(4,128)} %copy.7), calls=%async_computation.1 | async-start | bytes 1048576 | tf_op jit(solution)/shard_map/all_to_all | solution.py:87
  196.7 264.5 %all-reduce.36.cloned.1.call-start = ((), (), s32[]{:S(2)}) async-start(), calls=%async_computation.3 | async-start | bytes 524288 | tf_op jit(solution)/shard_map/psum | solution.py:99
  214.2 247.0 %copy-start.3 = (f32[256,256]{1,0:T(8,128)S(1)}, f32[256,256]{1,0:T(8,128)}, u32[]{:S(2)}) copy-start(f32[256,256]{1,0:T(8,128)} %param.7) | copy-start | bytes 786436
Sparse Core Ops, SparseCore 0:
  215.7 245.4 all-reduce.35
